TPU v7x, 512 devices: a whole 4x8x8 slice. The times are simulated.
512 devices in a mesh: dp: 32 (over x, y_lo, core), mp: 16 (over z, y_hi).
Axes of the slice: x: 4, y: 8 (y_hi: 2, y_lo: 4; y = y_hi * 4 + y_lo), z: 8, core: 2. Of those that a mesh axis runs over, the one named last changes fastest.
Arguments:
- features: bfloat16 [57344, 1024], P(('dp', 'mp')), may hold values from -6 to 6
- row_position: int32 [57344], P(('dp', 'mp')), may hold values from 0 to 2047, as said below
- proj_weight: bfloat16 [1024, 8192], P(None, 'mp'), may hold values from -0.1875 to 0.1875
- proj_bias: float32 [8192], P('mp'), may hold values from -3 to 3
- norm_gain: float32 [8192], replicated, may hold values from 0.5 to 1.5
- cotangent: bfloat16 [65536, 8192], P(('dp', 'mp')), may hold values from -0.03125 to 0.03125
Outputs:
- grad_weight: bfloat16 [1024, 8192], P(None, 'mp')
- grad_bias: float32 [8192], P('mp')
Inputs may be any that keep to these rules, and one draw needn't show every extreme that they name: `row_position`: within each sequence's block of 1792 entries the positions are distinct; every such block holds position 0 and position 2047.
All inputs are finite; a program needn't handle non-finite values.
Results may differ from a plain program's by a relative error of at most 0.0059.
Values may be sent and summed in bfloat16 or wider, within the bound.
No kernel may reach another device: no remote copies, remote signals or barrier semaphores. Data moves between devices by JAX's collectives and lax.ppermute only.
A program may use at most 64 MiB of HBM per device.

v0:
```python
import jax
import jax.numpy as jnp
from jax import lax
from jax.sharding import PartitionSpec as P

EPSILON = 1e-05


def gelu_pair(pre_act):
    normal_cdf = 0.5 * (1.0 + lax.erf(pre_act * 0.7071067811865476))
    normal_pdf = jnp.exp(-0.5 * pre_act * pre_act) * 0.3989422804014327
    return (pre_act * normal_cdf, normal_cdf + pre_act * normal_pdf)


def per_device(features, row_position, proj_weight, proj_bias, norm_gain, cotangent):
    width = proj_weight.shape[1]
    seq_len = cotangent.shape[0] * lax.axis_size("mp")
    places = lax.all_gather(row_position, "mp", axis=0, tiled=True)
    total = places.shape[0]
    all_feats = lax.all_gather(features, "mp", axis=0, tiled=True)
    pre_act = jnp.dot(all_feats, proj_weight, preferred_element_type=jnp.float32) + proj_bias
    activated, slope = gelu_pair(pre_act)
    projected = activated.astype(jnp.bfloat16)
    source = (
        jnp.full((seq_len,), total, jnp.int32).at[places].set(jnp.arange(total, dtype=jnp.int32))
    )
    padded = jnp.concatenate([projected, jnp.zeros((1, width), jnp.bfloat16)], axis=0)
    outgoing = padded[source]
    embed = lax.all_to_all(outgoing, "mp", split_axis=0, concat_axis=1, tiled=True)
    embed_wide = lax.optimization_barrier(embed).astype(jnp.float32)
    inv_rms = lax.rsqrt(jnp.mean(embed_wide * embed_wide, axis=1, keepdims=True) + EPSILON)
    scaled_cot = cotangent.astype(jnp.float32) * norm_gain
    gdot = jnp.mean(scaled_cot * embed_wide, axis=1, keepdims=True)
    grad_embed = (inv_rms * scaled_cot - embed_wide * inv_rms * inv_rms * inv_rms * gdot).astype(
        jnp.bfloat16
    )
    returned = lax.all_to_all(grad_embed, "mp", split_axis=1, concat_axis=0, tiled=True)
    grad_proj = lax.optimization_barrier(returned[places]).astype(jnp.float32)
    grad_pre = (grad_proj * slope).astype(jnp.bfloat16)
    bias_grad = jnp.sum(grad_pre.astype(jnp.float32), axis=0)
    weight_grad = lax.dot_general(
        all_feats, grad_pre, (((0,), (0,)), ((), ())), preferred_element_type=jnp.float32
    )
    weight_grad, bias_grad = lax.psum((weight_grad, bias_grad), "dp")
    return (weight_grad.astype(jnp.bfloat16), bias_grad)


def solution(mesh):
    return jax.shard_map(
        per_device,
        mesh=mesh,
        in_specs=(
            P(("dp", "mp"), None),
            P(("dp", "mp")),
            P(None, "mp"),
            P("mp"),
            P(),
            P(("dp", "mp"), None),
        ),
        out_specs=(P(None, "mp"), P("mp")),
        check_vma=False,
    )
```

profile of v0, /device:TPU:64, one launch (start us, length us, event | category | flops | bytes accessed | tf_op | source)
XLA Modules:
  0.0 493.4 jit_solution(16986138296196837244)
XLA Ops:
  7.2 0.0 copy-start
  7.2 0.0 all-gather.2.cloned.1.call-start
  7.2 0.7 all-gather.2.cloned.1.call-update
  7.9 1.3 dynamic-slice
  9.8 0.9 dynamic-update-slice
  10.7 24.4 %all-reduce.1 = s32[1792]{0:T(1024)S(1)} all-reduce(s32[1792]{0:T(1024)S(1)} %dynamic-update-slice), channel_id=1, replica_groups=mesh['dp'=32,'mp'=16] {'mp'}, use_global_device_ids=true, to_apply=%add.1 | all-reduce | flops 1792 | bytes 14336
  35.1 7.1 %scatter_custom_fusion = s32[2048]{0:T(1024)S(1)} fusion(s32[1792]{0:T(1024)S(1)} %compare_select_fusion.1, s32[1792]{0:T(1024)S(1)} %iota.3, s32[]{:T(128)} %constant.5.clone.1), kind=kCustom, calls=%fused_computation.30 | custom fusion | bytes 8196 | tf_op jit(solution)/shard_map/scatter | solution.py:25
  42.3 98.6 %all-gather.2.cloned.1.call-done = bf16[1792,1024]{1,0:T(8,128)(2,1)} async-done(((bf16[112,1024]{1,0:T(8,128)(2,1)}), bf16[1792,1024]{1,0:T(8,128)(2,1)}) %all-gather.2.cloned.1.call-update) | async-done | bytes 3670032 | tf_op jit(solution)/shard_map/all_gather | solution.py:20
  140.9 0.0 copy-done
  140.9 5.9 %multiply_convert_fusion = (bf16[1792,512]{1,0:T(8,128)(2,1)S(1)}, f32[1792,512]{1,0:T(8,128)}) fusion(f32[512]{0:T(512)} %param.9, bf16[1792,1024]{1,0:T(8,128)(2,1)} %all-gather.2.cloned.1.call-done, bf16[1024,512]{1,0:T(8,128)(2,1)S(1)} %copy-done), kind=kOutput, calls=%fused_computation.22 | convolution fusion | flops 1884553216 | bytes 10225664 | tf_op jit(solution)/shard_map/dot_general | solution.py:21
  146.7 0.1 concatenate.3
  146.8 9.2 %gather_fusion = bf16[2048,512]{1,0:T(8,128)(2,1)} fusion(bf16[1793,512]{1,0:T(8,128)(2,1)S(1)} %concatenate.3, s32[2048]{0:T(1024)S(1)} %fusion.13), kind=kCustom, calls=%fused_computation | custom fusion | bytes 4202496 | tf_op jit(solution)/shard_map/gather | solution.py:28
  156.0 0.0 copy-start.1
  156.0 0.0 copy-start.2
  156.0 47.0 %all_to_all.38 = bf16[16,128,512]{2,1,0:T(8,128)(2,1)S(1)} all-to-all(bf16[16,128,512]{2,1,0:T(8,128)(2,1)} %bitcast.22), channel_id=1, replica_groups=mesh['dp'=32,'mp'=16] {'mp'}, dimensions={0} | all-to-all | bytes 4194304 | tf_op jit(solution)/shard_map/all_to_all | solution.py:29
  203.0 0.2 copy.12
  203.2 0.0 copy-done.1
  203.3 0.0 copy-done.2
  203.3 1.1 fusion
  204.4 1.4 fusion.5
  205.8 1.6 copy.14
  207.5 10.0 %all-to-all-start.1 = ((bf16[128,16,512]{2,0,1:T(8,128)(2,1)}), bf16[128,16,512]{2,0,1:T(8,128)(2,1)S(1)}, u32[]{:S(2)}, u32[]{:S(2)}) async-start(bf16[128,16,512]{2,0,1:T(8,128)(2,1)} %bitcast.23), calls=%async_computation.1 | async-start | bytes 4194304 | tf_op jit(solution)/shard_map/all_to_all | solution.py:37
  217.5 54.2 %all-to-all-done.1 = bf16[128,16,512]{2,0,1:T(8,128)(2,1)S(1)} async-done(((bf16[128,16,512]{2,0,1:T(8,128)(2,1)}), bf16[128,16,512]{2,0,1:T(8,128)(2,1)S(1)}, u32[]{:S(2)}, u32[]{:S(2)}) %all-to-all-start.1) | async-done | bytes 2097184 | tf_op jit(solution)/shard_map/all_to_all | solution.py:37
  271.8 0.0 copy-start.3
  271.8 6.1 %gather_fusion.1 = bf16[1792,512]{1,0:T(8,128)(2,1)} fusion(bf16[2048,512]{1,0:T(8,128)(2,1)S(1)} %bitcast.19, s32[2048]{0:T(1024)S(1)} %pad_clamp_fusion), kind=kCustom, calls=%fused_computation.1 | custom fusion | bytes 3677184 | tf_op jit(solution)/shard_map/gather | solution.py:38
  277.9 0.0 copy-done.3
  277.9 0.0 copy-start.4
  277.9 3.8 convert_reduce_fusion
  281.7 0.0 copy-done.4
  281.7 2.1 convolution_bitcast_fusion
  283.8 200.5 %all-reduce.4 = (bf16[1024,512]{0,1:T(8,128)(2,1)}, f32[512]{0:T(512)}) all-reduce(f32[1024,512]{0,1:T(8,128)S(1)} %convolution_bitcast_fusion, f32[512]{0:T(512)S(1)} %get-tuple-element.8), channel_id=1, replica_groups=mesh['dp'=32,'mp'=16] {'dp'}, use_global_device_ids=true, to_apply=%region_3.0 | all-reduce | flops 524800 | bytes 3149824 | tf_op jit(solution)/shard_map/psum | solution.py:44
  484.3 2.3 copy.10
  (6 shorter events, 0.0 us)
Async XLA Ops:
  7.2 133.7 %copy-start = (bf16[1024,512]{1,0:T(8,128)(2,1)S(1)}, bf16[1024,512]{1,0:T(8,128)(2,1)}, u32[]{:S(2)}) copy-start(bf16[1024,512]{1,0:T(8,128)(2,1)} %param.8) | copy-start | bytes 3145732
  7.2 133.7 %all-gather.2.cloned.1.call-start = ((), (), s32[]{:S(2)}) async-start(), calls=%async_computation.2 | async-start | bytes 3899392 | tf_op jit(solution)/shard_map/all_gather | solution.py:20
  156.0 47.3 %copy-start.1 = (bf16[128,8192]{1,0:T(8,128)(2,1)S(1)}, bf16[128,8192]{1,0:T(8,128)(2,1)}, u32[]{:S(2)}) copy-start(bf16[128,8192]{1,0:T(8,128)(2,1)} %param.11) | copy-start | bytes 6291460
  156.0 47.3 %copy-start.2 = (f32[8192]{0:T(1024)S(1)}, f32[8192]{0:T(1024)}, u32[]{:S(2)}) copy-start(f32[8192]{0:T(1024)} %param.10) | copy-start | bytes 98308
  207.5 64.3 %all-to-all-start.1 = ((bf16[128,16,512]{2,0,1:T(8,128)(2,1)}), bf16[128,16,512]{2,0,1:T(8,128)(2,1)S(1)}, u32[]{:S(2)}, u32[]{:S(2)}) async-start(bf16[128,16,512]{2,0,1:T(8,128)(2,1)} %bitcast.23), calls=%async_computation.1 | async-start | bytes 4194304 | tf_op jit(solution)/shard_map/all_to_all | solution.py:37
  271.8 6.1 %copy-start.3 = (f32[512]{0:T(512)S(1)}, f32[512]{0:T(512)}, u32[]{:S(2)}) copy-start(f32[512]{0:T(512)} %param.9) | copy-start | bytes 6148
  277.9 3.8 copy-start.4
Sparse Core Ops, SparseCore 0:
  11.2 129.6 all-gather.1
where the time goes:
time: 494 us; the launch traced here: 493 us
  blocking collectives  272 us (55%)
  waiting for transfers between devices  154 us (31%)
  local copies, waits for them, and re-layouts  28.8 us (6%)
  between operations  14.8 us (3%)
  starting transfers between devices  10.1 us (2%)
  matrix products  7.94 us (2%)
  other arithmetic  6.38 us (1%)
    psum x1, blocking collectives, per_device(): weight_grad, bias_grad = lax.psum((weight_grad, bias_grad), 'dp')  201 us
    all_gather x1, waiting for transfers between devices, per_device(): all_feats = lax.all_gather(features, 'mp', axis=0, tiled=True)  98.6 us
    all_to_all x1, waiting for transfers between devices, per_device(): lax.all_to_all(grad_embed, 'mp', split_axis=1, concat_axis=0, tiled=True)  54.2 us
    all_to_all x1, blocking collectives, per_device(): lax.all_to_all(outgoing, 'mp', split_axis=0, concat_axis=1, tiled=True)  47 us
    unnamed x1, blocking collectives  24.4 us
    all_to_all x1, starting transfers between devices, per_device(): lax.all_to_all(grad_embed, 'mp', split_axis=1, concat_axis=0, tiled=True)  10 us
  transfers between devices with their start and end apart: 2, of which 2 were waited for; matrix products, arithmetic and copies ran while one was open for 2% of the time, Pallas kernels for 0%

commit v1 on v0

--- a/solution.py
+++ b/solution.py
@@ -34,7 +34,10 @@
     grad_embed = (inv_rms * scaled_cot - embed_wide * inv_rms * inv_rms * inv_rms * gdot).astype(
         jnp.bfloat16
     )
-    returned = lax.all_to_all(grad_embed, "mp", split_axis=1, concat_axis=0, tiled=True)
+    returned = jnp.concatenate(
+        lax.all_to_all(jnp.stack(jnp.split(grad_embed, lax.axis_size("mp"), axis=1)), "mp", 0, 0),
+        axis=0,
+    )
     grad_proj = lax.optimization_barrier(returned[places]).astype(jnp.float32)
     grad_pre = (grad_proj * slope).astype(jnp.bfloat16)
     bias_grad = jnp.sum(grad_pre.astype(jnp.float32), axis=0)

time: 494 us -> 504 us (1.020)
  local copies, waits for them, and re-layouts: 28.8 us -> 39 us
    unnamed x14 -> x29, local copies, waits for them, and re-layouts: 4.44 us -> 15.6 us
where the time goes in v1:
time: 504 us
  blocking collectives  272 us (54%)
  waiting for transfers between devices  154 us (31%)
  local copies, waits for them, and re-layouts  39 us (8%)
  between operations  14.8 us (3%)
  starting transfers between devices  10.1 us (2%)
  matrix products  7.94 us (2%)
  other arithmetic  6.38 us (1%)
    psum x1, blocking collectives, per_device(): weight_grad, bias_grad = lax.psum((weight_grad, bias_grad), 'dp')  201 us
    all_gather x1, waiting for transfers between devices, per_device(): all_feats = lax.all_gather(features, 'mp', axis=0, tiled=True)  98.6 us
    all_to_all x1, waiting for transfers between devices, per_device(): lax.all_to_all(jnp.stack(jnp.split(grad_embed, lax.axis_size('mp'), axis=...  54.2 us
    all_to_all x1, blocking collectives, per_device(): lax.all_to_all(outgoing, 'mp', split_axis=0, concat_axis=1, tiled=True)  46.9 us
    unnamed x1, blocking collectives  24.4 us
    unnamed x29, local copies, waits for them, and re-layouts  15.6 us
  transfers between devices with their start and end apart: 2, of which 2 were waited for; matrix products, arithmetic and copies ran while one was open for 2% of the time, Pallas kernels for 0%

profile of v1, /device:TPU:64, one launch (start us, length us, event | category | flops | bytes accessed | tf_op | source)
XLA Modules:
  0.0 503.5 jit_solution(17934256153847902769)
XLA Ops:
  7.2 0.0 copy-start
  7.2 0.0 all-gather.2.cloned.1.call-start
  7.2 0.7 all-gather.2.cloned.1.call-update
  7.9 1.3 dynamic-slice
  9.8 0.9 dynamic-update-slice
  10.7 24.4 %all-reduce.1 = s32[1792]{0:T(1024)S(1)} all-reduce(s32[1792]{0:T(1024)S(1)} %dynamic-update-slice), channel_id=1, replica_groups=mesh['dp'=32,'mp'=16] {'mp'}, use_global_device_ids=true, to_apply=%add.1 | all-reduce | flops 1792 | bytes 14336
  35.1 7.1 %scatter_custom_fusion = s32[2048]{0:T(1024)S(1)} fusion(s32[1792]{0:T(1024)S(1)} %compare_select_fusion.1, s32[1792]{0:T(1024)S(1)} %iota.3, s32[]{:T(128)} %constant.5.clone.1), kind=kCustom, calls=%fused_computation.61 | custom fusion | bytes 8196 | tf_op jit(solution)/shard_map/scatter | solution.py:25
  42.3 98.6 %all-gather.2.cloned.1.call-done = bf16[1792,1024]{1,0:T(8,128)(2,1)} async-done(((bf16[112,1024]{1,0:T(8,128)(2,1)}), bf16[1792,1024]{1,0:T(8,128)(2,1)}) %all-gather.2.cloned.1.call-update) | async-done | bytes 3670032 | tf_op jit(solution)/shard_map/all_gather | solution.py:20
  140.9 0.0 copy-done
  140.9 5.9 %multiply_convert_fusion = (bf16[1792,512]{1,0:T(8,128)(2,1)S(1)}, f32[1792,512]{1,0:T(8,128)}) fusion(f32[512]{0:T(512)} %param.9, bf16[1792,1024]{1,0:T(8,128)(2,1)} %all-gather.2.cloned.1.call-done, bf16[1024,512]{1,0:T(8,128)(2,1)S(1)} %copy-done), kind=kOutput, calls=%fused_computation.22 | convolution fusion | flops 1884553216 | bytes 10225664 | tf_op jit(solution)/shard_map/dot_general | solution.py:21
  146.7 0.1 concatenate.3
  146.8 9.2 %gather_fusion = bf16[2048,512]{1,0:T(8,128)(2,1)} fusion(bf16[1793,512]{1,0:T(8,128)(2,1)S(1)} %concatenate.3, s32[2048]{0:T(1024)S(1)} %fusion.29), kind=kCustom, calls=%fused_computation | custom fusion | bytes 4202496 | tf_op jit(solution)/shard_map/gather | solution.py:28
  156.0 46.9 %all_to_all.24 = bf16[16,128,512]{2,1,0:T(8,128)(2,1)S(1)} all-to-all(bf16[16,128,512]{2,1,0:T(8,128)(2,1)} %bitcast.80), channel_id=1, replica_groups=mesh['dp'=32,'mp'=16] {'mp'}, dimensions={0} | all-to-all | bytes 4194304 | tf_op jit(solution)/shard_map/all_to_all | solution.py:29
  202.9 0.0 copy-start.1
  202.9 0.0 copy-start.2
  202.9 0.2 copy.10
  203.1 1.4 copy-done.1
  204.5 0.0 copy-done.2
  204.5 1.1 fusion
  205.6 1.4 fusion.5
  207.1 0.7 fusion.28
  207.7 0.7 fusion.27
  208.4 0.7 fusion.26
  209.0 0.6 fusion.25
  209.7 0.6 fusion.24
  210.3 0.7 fusion.23
  211.0 0.7 fusion.22
  211.6 0.7 fusion.21
  212.3 0.7 fusion.20
  213.0 0.6 fusion.19
  213.6 0.7 fusion.18
  214.3 0.6 fusion.17
  214.9 0.7 fusion.16
  215.6 0.7 fusion.15
  216.2 0.7 fusion.14
  216.9 0.7 fusion.13
  217.6 10.0 %all-to-all-start.1 = ((bf16[16,128,512]{2,1,0:T(8,128)(2,1)}), bf16[16,128,512]{2,1,0:T(8,128)(2,1)S(1)}, u32[]{:S(2)}, u32[]{:S(2)}) async-start(bf16[16,128,512]{2,1,0:T(8,128)(2,1)} %fusion.13), calls=%async_computation.1 | async-start | bytes 4194304 | tf_op jit(solution)/shard_map/all_to_all | solution.py:38
  227.6 54.2 %all-to-all-done.1 = bf16[16,128,512]{2,1,0:T(8,128)(2,1)S(1)} async-done(((bf16[16,128,512]{2,1,0:T(8,128)(2,1)}), bf16[16,128,512]{2,1,0:T(8,128)(2,1)S(1)}, u32[]{:S(2)}, u32[]{:S(2)}) %all-to-all-start.1) | async-done | bytes 2097184 | tf_op jit(solution)/shard_map/all_to_all | solution.py:38
  281.9 0.0 copy-start.3
  281.9 6.1 %gather_fusion.1 = bf16[1792,512]{1,0:T(8,128)(2,1)} fusion(bf16[2048,512]{1,0:T(8,128)(2,1)S(1)} %bitcast.77, s32[2048]{0:T(1024)S(1)} %pad_clamp_fusion), kind=kCustom, calls=%fused_computation.1 | custom fusion | bytes 3677184 | tf_op jit(solution)/shard_map/gather | solution.py:41
  288.0 0.0 copy-done.3
  288.0 0.0 copy-start.4
  288.0 3.8 convert_reduce_fusion
  291.8 0.0 copy-done.4
  291.8 2.1 convolution_bitcast_fusion
  293.9 200.5 %all-reduce.4 = (bf16[1024,512]{0,1:T(8,128)(2,1)}, f32[512]{0:T(512)}) all-reduce(f32[1024,512]{0,1:T(8,128)S(1)} %convolution_bitcast_fusion, f32[512]{0:T(512)S(1)} %get-tuple-element.8), channel_id=1, replica_groups=mesh['dp'=32,'mp'=16] {'dp'}, use_global_device_ids=true, to_apply=%region_3.0 | all-reduce | flops 524800 | bytes 3149824 | tf_op jit(solution)/shard_map/psum | solution.py:47
  494.4 2.3 copy.9
  (6 shorter events, 0.0 us)
Async XLA Ops:
  7.2 133.7 %copy-start = (bf16[1024,512]{1,0:T(8,128)(2,1)S(1)}, bf16[1024,512]{1,0:T(8,128)(2,1)}, u32[]{:S(2)}) copy-start(bf16[1024,512]{1,0:T(8,128)(2,1)} %param.8) | copy-start | bytes 3145732
  7.2 133.7 %all-gather.2.cloned.1.call-start = ((), (), s32[]{:S(2)}) async-start(), calls=%async_computation.2 | async-start | bytes 3899392 | tf_op jit(solution)/shard_map/all_gather | solution.py:20
  202.9 1.6 copy-start.1
  202.9 1.6 copy-start.2
  217.6 64.3 %all-to-all-start.1 = ((bf16[16,128,512]{2,1,0:T(8,128)(2,1)}), bf16[16,128,512]{2,1,0:T(8,128)(2,1)S(1)}, u32[]{:S(2)}, u32[]{:S(2)}) async-start(bf16[16,128,512]{2,1,0:T(8,128)(2,1)} %fusion.13), calls=%async_computation.1 | async-start | bytes 4194304 | tf_op jit(solution)/shard_map/all_to_all | solution.py:38
  281.9 6.1 %copy-start.3 = (f32[512]{0:T(512)S(1)}, f32[512]{0:T(512)}, u32[]{:S(2)}) copy-start(f32[512]{0:T(512)} %param.9) | copy-start | bytes 6148
  288.0 3.8 copy-start.4
Sparse Core Ops, SparseCore 0:
  11.2 129.6 all-gather.1

commit v2 on v0

--- a/solution.py
+++ b/solution.py
@@ -17,7 +17,9 @@
     seq_len = cotangent.shape[0] * lax.axis_size("mp")
     places = lax.all_gather(row_position, "mp", axis=0, tiled=True)
     total = places.shape[0]
-    all_feats = lax.all_gather(features, "mp", axis=0, tiled=True)
+    all_feats = jnp.concatenate(
+        lax.all_to_all(jnp.stack([features] * lax.axis_size("mp")), "mp", 0, 0), axis=0
+    )
     pre_act = jnp.dot(all_feats, proj_weight, preferred_element_type=jnp.float32) + proj_bias
     activated, slope = gelu_pair(pre_act)
     projected = activated.astype(jnp.bfloat16)

time: 494 us -> 531 us (1.075)
  the two profiles are of different devices: /device:TPU:64 before, /device:TPU:32 now
where the time goes in v2:
time: 531 us; the launch traced here: 530 us
  blocking collectives  399 us (75%)
  waiting for transfers between devices  57 us (11%)
  local copies, waits for them, and re-layouts  31.5 us (6%)
  starting transfers between devices  24.9 us (5%)
  matrix products  10 us (2%)
  other arithmetic  6.23 us (1%)
    psum x1, blocking collectives, per_device(): weight_grad, bias_grad = lax.psum((weight_grad, bias_grad), 'dp')  239 us
    unnamed x1, blocking collectives  96.7 us
    all_to_all x1, blocking collectives, per_device(): lax.all_to_all(outgoing, 'mp', split_axis=0, concat_axis=1, tiled=True)  63.2 us
    all_to_all x1, waiting for transfers between devices, per_device(): lax.all_to_all(grad_embed, 'mp', split_axis=1, concat_axis=0, tiled=True)  57 us
    all_to_all x1, starting transfers between devices, per_device(): lax.all_to_all(jnp.stack([features] * lax.axis_size('mp')), 'mp', 0, 0)  15.8 us
  transfers between devices with their start and end apart: 2, of which 1 were waited for; matrix products, arithmetic and copies ran while one was open for 2% of the time, Pallas kernels for 0%

profile of v2, /device:TPU:32, one launch (start us, length us, event | category | flops | bytes accessed | tf_op | source)
XLA Modules:
  0.0 530.2 jit_solution(6733188319794304451)
XLA Ops:
  0.6 0.0 copy-start
  0.6 3.3 stack.2
  4.0 0.0 copy-start.4
  4.0 0.0 copy-start.3
  4.0 15.8 %all-to-all-start = ((bf16[16,112,1024]{2,1,0:T(8,128)(2,1)}), bf16[16,112,1024]{2,1,0:T(8,128)(2,1)}, u32[]{:S(2)}, u32[]{:S(2)}) async-start(bf16[16,112,1024]{2,1,0:T(8,128)(2,1)} %stack.2), calls=%async_computation | async-start | bytes 7340032 | tf_op jit(solution)/shard_map/all_to_all | solution.py:21
  19.8 1.3 dynamic-slice
  21.7 0.0 copy-done.4
  21.7 0.3 dynamic-update-slice
  22.0 96.7 %all-reduce.1 = s32[1792]{0:T(1024)S(1)} all-reduce(s32[1792]{0:T(1024)S(1)} %dynamic-update-slice), channel_id=1, replica_groups=mesh['dp'=32,'mp'=16] {'mp'}, use_global_device_ids=true, to_apply=%add.1 | all-reduce | flops 1792 | bytes 14336
  118.7 7.1 %scatter_custom_fusion = s32[2048]{0:T(1024)S(1)} fusion(s32[1792]{0:T(1024)S(1)} %compare_select_fusion.1, s32[1792]{0:T(1024)S(1)} %iota.3, s32[]{:T(128)} %constant.5.clone.1), kind=kCustom, calls=%fused_computation.30 | custom fusion | bytes 8196 | tf_op jit(solution)/shard_map/scatter | solution.py:27
  125.9 0.0 all-to-all-done
  125.9 0.0 copy-done
  125.9 0.0 copy-done.3
  125.9 5.8 %multiply_convert_fusion = (bf16[1792,512]{1,0:T(8,128)(2,1)S(1)}, f32[1792,512]{1,0:T(8,128)}) fusion(f32[512]{0:T(512)S(1)} %copy-done.3, bf16[1792,1024]{1,0:T(8,128)(2,1)} %bitcast, bf16[1024,512]{1,0:T(8,128)(2,1)S(1)} %copy-done), kind=kOutput, calls=%fused_computation.22 | convolution fusion | flops 1884553216 | bytes 10225664 | tf_op jit(solution)/shard_map/dot_general | solution.py:23
  131.7 0.1 concatenate.3
  131.8 9.2 %gather_fusion = bf16[2048,512]{1,0:T(8,128)(2,1)} fusion(bf16[1793,512]{1,0:T(8,128)(2,1)S(1)} %concatenate.3, s32[2048]{0:T(1024)S(1)} %fusion.13), kind=kCustom, calls=%fused_computation | custom fusion | bytes 4202496 | tf_op jit(solution)/shard_map/gather | solution.py:30
  141.0 0.0 copy-start.1
  141.0 0.0 copy-start.2
  141.0 63.2 %all_to_all.43 = bf16[16,128,512]{2,1,0:T(8,128)(2,1)S(1)} all-to-all(bf16[16,128,512]{2,1,0:T(8,128)(2,1)} %bitcast.23), channel_id=1, replica_groups=mesh['dp'=32,'mp'=16] {'mp'}, dimensions={0} | all-to-all | bytes 4194304 | tf_op jit(solution)/shard_map/all_to_all | solution.py:31
  204.2 0.2 copy.12
  204.4 0.0 copy-done.1
  204.4 0.0 copy-done.2
  204.4 1.1 fusion
  205.6 1.4 fusion.5
  207.0 1.6 copy.14
  208.6 9.0 %all-to-all-start.2 = ((bf16[128,16,512]{2,0,1:T(8,128)(2,1)}), bf16[128,16,512]{2,0,1:T(8,128)(2,1)S(1)}, u32[]{:S(2)}, u32[]{:S(2)}) async-start(bf16[128,16,512]{2,0,1:T(8,128)(2,1)} %bitcast.24), calls=%async_computation.2 | async-start | bytes 4194304 | tf_op jit(solution)/shard_map/all_to_all | solution.py:39
  217.7 57.0 %all-to-all-done.2 = bf16[128,16,512]{2,0,1:T(8,128)(2,1)S(1)} async-done(((bf16[128,16,512]{2,0,1:T(8,128)(2,1)}), bf16[128,16,512]{2,0,1:T(8,128)(2,1)S(1)}, u32[]{:S(2)}, u32[]{:S(2)}) %all-to-all-start.2) | async-done | bytes 2097184 | tf_op jit(solution)/shard_map/all_to_all | solution.py:39
  274.6 6.1 %gather_fusion.1 = bf16[1792,512]{1,0:T(8,128)(2,1)} fusion(bf16[2048,512]{1,0:T(8,128)(2,1)S(1)} %bitcast.20, s32[2048]{0:T(1024)S(1)} %pad_clamp_fusion), kind=kCustom, calls=%fused_computation.1 | custom fusion | bytes 3677184 | tf_op jit(solution)/shard_map/gather | solution.py:40
  280.8 3.6 convert_reduce_fusion
  284.4 4.2 convolution_bitcast_fusion
  288.6 239.4 %all-reduce.4 = (bf16[1024,512]{0,1:T(8,128)(2,1)}, f32[512]{0:T(512)}) all-reduce(f32[1024,512]{0,1:T(8,128)S(1)} %convolution_bitcast_fusion, f32[512]{0:T(512)S(1)} %get-tuple-element.8), channel_id=1, replica_groups=mesh['dp'=32,'mp'=16] {'dp'}, use_global_device_ids=true, to_apply=%region_3.0 | all-reduce | flops 524800 | bytes 3149824 | tf_op jit(solution)/shard_map/psum | solution.py:46
  527.9 2.3 copy.10
  (6 shorter events, 0.0 us)
Async XLA Ops:
  0.6 125.2 %copy-start = (bf16[1024,512]{1,0:T(8,128)(2,1)S(1)}, bf16[1024,512]{1,0:T(8,128)(2,1)}, u32[]{:S(2)}) copy-start(bf16[1024,512]{1,0:T(8,128)(2,1)} %param.8) | copy-start | bytes 3145732
  4.0 17.8 %copy-start.4 = (s32[112]{0:T(128)S(1)}, s32[112]{0:T(128)}, u32[]{:S(2)}) copy-start(s32[112]{0:T(128)} %param.7) | copy-start | bytes 1348
  4.0 121.9 %copy-start.3 = (f32[512]{0:T(512)S(1)}, f32[512]{0:T(512)}, u32[]{:S(2)}) copy-start(f32[512]{0:T(512)} %param.9) | copy-start | bytes 6148
  4.0 121.9 %all-to-all-start = ((bf16[16,112,1024]{2,1,0:T(8,128)(2,1)}), bf16[16,112,1024]{2,1,0:T(8,128)(2,1)}, u32[]{:S(2)}, u32[]{:S(2)}) async-start(bf16[16,112,1024]{2,1,0:T(8,128)(2,1)} %stack.2), calls=%async_computation | async-start | bytes 7340032 | tf_op jit(solution)/shard_map/all_to_all | solution.py:21
  141.0 63.4 %copy-start.1 = (bf16[128,8192]{1,0:T(8,128)(2,1)S(1)}, bf16[128,8192]{1,0:T(8,128)(2,1)}, u32[]{:S(2)}) copy-start(bf16[128,8192]{1,0:T(8,128)(2,1)} %param.11) | copy-start | bytes 6291460
  141.0 63.4 %copy-start.2 = (f32[8192]{0:T(1024)S(1)}, f32[8192]{0:T(1024)}, u32[]{:S(2)}) copy-start(f32[8192]{0:T(1024)} %param.10) | copy-start | bytes 98308
  208.6 66.0 %all-to-all-start.2 = ((bf16[128,16,512]{2,0,1:T(8,128)(2,1)}), bf16[128,16,512]{2,0,1:T(8,128)(2,1)S(1)}, u32[]{:S(2)}, u32[]{:S(2)}) async-start(bf16[128,16,512]{2,0,1:T(8,128)(2,1)} %bitcast.24), calls=%async_computation.2 | async-start | bytes 4194304 | tf_op jit(solution)/shard_map/all_to_all | solution.py:39
